TPU v7x, 128 devices: a whole 4x4x4 slice. The times are simulated.
128 devices in a mesh: grp: 4 (over z), tok: 32 (over y, x, core).
Axes of the slice: x: 4, y: 4, z: 4, core: 2. Of those that a mesh axis runs over, the one named last changes fastest.
Arguments:
- tokens: bfloat16 [32768, 1408], P(('grp', 'tok')), may hold values from -6 to 6
- seg_ids: int32 [32768], P(('grp', 'tok')), may hold values from 0 to 8191, as said below
- merge_index: int32 [32768], P(('grp', 'tok')), may hold values from 0 to 255, as said below
- owners: int32 [8192, 1], P(('grp', 'tok')), may hold values from 0 to 31; in each aligned block of 64 rows (0 to 63, 64 to 127, ...) at most 4 rows name the same one
- w_qkv: bfloat16 [1408, 2112], replicated, may hold values from -0.15625 to 0.15625
- w_attn_out: bfloat16 [704, 1408], replicated, may hold values from -1.75 to 1.75
- w_in: bfloat16 [6144, 1408], P('grp'), may hold values from -0.15625 to 0.15625
- in_bias: bfloat16 [6144], P('grp'), may hold values from -3 to 3
- w_out: bfloat16 [6144, 1408], P('grp'), may hold values from -0.078125 to 0.078125
- out_bias: float32 [1408], replicated, may hold values from -3 to 3
- merge_gain: float32 [1408], replicated, may hold values from 0.1 to 1.9
- w_merge: bfloat16 [5632, 2048], P(None, 'grp'), may hold values from -0.078125 to 0.078125
- merge_bias: float32 [2048], P('grp'), may hold values from -3 to 3
Outputs:
- embeds: bfloat16 [16384, 2048], P('tok', 'grp')
Inputs may be any that keep to these rules, and one draw needn't show every extreme that they name: `seg_ids`: never falling along the tokens; every segment starts at a multiple of 4 tokens, has a multiple of 4 tokens and lies within one aligned block of 8192 tokens. `merge_index`: in each aligned block of 256 entries the values are a permutation of 0 to 255, and each aligned group of 4 entries names rows of a single segment. `owners`: among the 64 merged tokens of one device no owner is named more than 4 times.
All inputs are finite; a program needn't handle non-finite values.
Results may differ from a plain program's by a relative error of at most 0.014.
Values may be sent and summed in bfloat16 or wider, within the bound.
No kernel may reach another device: no remote copies, remote signals or barrier semaphores. Data moves between devices by JAX's collectives and lax.ppermute only.
A program may use at most 320 MiB of HBM per device.

v0:
```python
import math
import jax
import jax.numpy as jnp
from jax import lax
from jax.sharding import PartitionSpec as P

HEADS = 8
HD = 88
NORM_EPS = 1e-06


def layer_norm(values):
    centred = values - jnp.mean(values, axis=-1, keepdims=True)
    return centred * lax.rsqrt(jnp.mean(centred * centred, axis=-1, keepdims=True) + NORM_EPS)


def head_norm(values):
    return values * lax.rsqrt(jnp.mean(values * values, axis=-1, keepdims=True) + NORM_EPS)


def local(
    tokens,
    seg_ids,
    merge_index,
    owners,
    w_qkv,
    w_attn_out,
    w_in,
    in_bias,
    w_out,
    out_bias,
    merge_gain,
    w_merge,
    merge_bias,
):
    tok_rows = tokens.shape[0]
    feat_width = tokens.shape[1]
    head_width = HEADS * HD
    normed = layer_norm(tokens.astype(jnp.float32)).astype(jnp.bfloat16)
    projected = jnp.dot(normed, w_qkv, preferred_element_type=jnp.float32).astype(jnp.bfloat16)
    queries = head_norm(
        projected[:, :head_width].astype(jnp.float32).reshape(tok_rows, HEADS, HD)
    ).astype(jnp.bfloat16)
    key_rows = head_norm(
        projected[:, head_width : 2 * head_width].astype(jnp.float32).reshape(tok_rows, HEADS, HD)
    ).astype(jnp.bfloat16)
    keys_values = jnp.concatenate(
        [key_rows.reshape(tok_rows, head_width), projected[:, 2 * head_width :]], axis=1
    )
    score_scale = 1.0 / math.sqrt(HD)
    piece_kv = lax.all_gather(keys_values, "tok", axis=0, tiled=True)
    piece_seg = lax.all_gather(seg_ids, "tok", axis=0, tiled=True)
    row_count = piece_kv.shape[0]
    piece_keys = piece_kv[:, :head_width].reshape(row_count, HEADS, HD)
    piece_values = piece_kv[:, head_width:].reshape(row_count, HEADS, HD)
    scores = (
        jnp.einsum("qhd,khd->hqk", queries, piece_keys, preferred_element_type=jnp.float32)
        * score_scale
    )
    same_segment = (seg_ids[:, None] == piece_seg[None, :])[None]
    weights = jnp.where(same_segment, jnp.exp(scores), 0.0)
    denominator = jnp.sum(weights, axis=-1)
    numerator = jnp.einsum(
        "hqk,khd->qhd",
        weights.astype(jnp.bfloat16),
        piece_values,
        preferred_element_type=jnp.float32,
    )
    numerator, denominator = (numerator, denominator)
    attended = (
        (numerator / jnp.transpose(denominator)[:, :, None])
        .astype(jnp.bfloat16)
        .reshape(tok_rows, head_width)
    )
    residual = (
        tokens.astype(jnp.float32)
        + jnp.dot(attended, w_attn_out, preferred_element_type=jnp.float32)
    ).astype(jnp.bfloat16)
    mlp_in = layer_norm(residual.astype(jnp.float32)).astype(jnp.bfloat16)
    pre_act = lax.dot_general(
        lax.all_gather(mlp_in, "grp", axis=0, tiled=True),
        w_in,
        (((1,), (1,)), ((), ())),
        preferred_element_type=jnp.float32,
    )
    hidden = jax.nn.gelu(pre_act + in_bias.astype(jnp.float32), approximate=False).astype(
        jnp.bfloat16
    )
    mlp_sum = lax.psum_scatter(
        jnp.dot(hidden, w_out, preferred_element_type=jnp.float32).astype(jnp.bfloat16),
        "grp",
        scatter_dimension=0,
        tiled=True,
    ).astype(jnp.float32)
    normed_out = (
        layer_norm(residual.astype(jnp.float32) + mlp_sum + out_bias) * merge_gain
    ).astype(jnp.bfloat16)
    merged_count = tok_rows // 4
    merged = jnp.take(normed_out, merge_index, axis=0).reshape(merged_count, 4 * feat_width)
    tok_devices = lax.axis_size("tok")
    grp_devices = lax.axis_size("grp")
    slot_cap = max(2, 2 * merged_count // tok_devices)
    owner_col = owners[:, 0]
    positions = jnp.arange(merged_count, dtype=jnp.int32)
    earlier = (owner_col[:, None] == owner_col[None, :]) & (positions[None, :] < positions[:, None])
    owner_rank = jnp.sum(earlier.astype(jnp.int32), axis=1)
    slot_index = owner_col * slot_cap + owner_rank
    merged_all, slots_all = (
        lax.all_gather(merged, "grp", axis=0, tiled=True),
        lax.all_gather(slot_index, "grp", axis=0, tiled=True),
    )
    embedded = (
        jnp.dot(merged_all, w_merge, preferred_element_type=jnp.float32) + merge_bias
    ).astype(jnp.bfloat16)
    out_cols = embedded.shape[1]
    slot_range = jnp.arange(tok_devices * slot_cap, dtype=jnp.int32)
    placement = (
        slots_all.reshape(grp_devices, 1, merged_count) == slot_range[None, :, None]
    ).astype(jnp.bfloat16)
    placement = placement.reshape(grp_devices, tok_devices, slot_cap, merged_count)
    outgoing = jnp.einsum(
        "gjrm,gmc->jgrc",
        placement,
        embedded.reshape(grp_devices, merged_count, out_cols),
        preferred_element_type=jnp.float32,
    ).astype(jnp.bfloat16)
    received = lax.all_to_all(outgoing, "tok", split_axis=0, concat_axis=2, tiled=True)
    return received.reshape(grp_devices * tok_devices * slot_cap, out_cols)


def solution(mesh):
    placed = (
        P(("grp", "tok"), None),
        P(("grp", "tok")),
        P(("grp", "tok")),
        P(("grp", "tok"), None),
        P(),
        P(),
        P("grp", None),
        P("grp"),
        P("grp", None),
        P(),
        P(),
        P(None, "grp"),
        P("grp"),
    )
    return jax.shard_map(
        local, mesh=mesh, in_specs=placed, out_specs=P("tok", "grp"), check_vma=False
    )
```

profile of v0, /device:TPU:1, one launch (start us, length us, event | category | flops | bytes accessed | tf_op | source)
XLA Modules:
  0.0 376.1 jit_solution(4948535860461258292)
XLA Ops:
  6.5 1.4 convert_reduce_fusion
  8.0 1.4 fusion.21
  9.4 4.9 %convolution_convert_fusion = bf16[256,2112]{0,1:T(8,128)(2,1)S(1)} fusion(bf16[1408,2112]{0,1:T(8,128)(2,1)} %param.17, bf16[256,1408]{1,0:T(8,128)(2,1)} %param.13, f32[256]{0:T(256)S(1)} %add_rsqrt_fusion.4, f32[256]{0:T(256)S(1)} %broadcast_multiply_fusion.2), kind=kOutput, calls=%fused_computation.28 | convolution fusion | flops 1524514816 | bytes 7751680 | tf_op jit(solution)/shard_map/dot_general | solution.py:40
  14.4 0.9 copy-done.2
  15.5 1.1 fusion.34
  16.5 0.9 pad_maximum_fusion
  17.5 26.0 %all-gather = s32[32,1,256]{2,1,0:T(1,128)S(1)} all-gather(s32[1,1,256]{2,1,0:T(1,128)S(1)} %bitcast.54), channel_id=1, replica_groups=mesh['grp'=4,'tok'=32] {'tok'}, dimensions={0}, use_global_device_ids=true | all-gather | bytes 33792 | tf_op jit(solution)/shard_map/all_gather | solution.py:52
  43.6 2.5 broadcast_compare_fusion
  46.1 72.6 %all-gather.5.cloned.1.call-done = bf16[8192,1408]{0,1:T(8,128)(2,1)} async-done(((bf16[256,1408]{0,1:T(8,128)(2,1)}), bf16[8192,1408]{0,1:T(8,128)(2,1)}) %all-gather.5.cloned.1.call-update) | async-done | bytes 23068688 | tf_op jit(solution)/shard_map/all_gather | solution.py:51
  118.7 16.6 %fusion.80 = (bf16[8192,704]{0,1:T(8,128)(2,1)}, bf16[8192,704]{0,1:T(8,128)(2,1)}) fusion(bf16[8192,1408]{0,1:T(8,128)(2,1)} %all-gather.5.cloned.1.call-done), kind=kLoop, calls=%fused_computation.116 | loop fusion | bytes 46137344 | tf_op jit(solution)/shard_map/slice | solution.py:54
  135.3 32.1 %fusion = (f32[8,256]{1,0:T(8,128)S(1)}, f32[8,256,8192]{2,1,0:T(8,128)}) fusion(pred[256,8192]{1,0:T(8,128)(4,1)} %broadcast_compare_fusion, bf16[8192,8,88]{0,2,1:T(8,128)(2,1)} %bitcast.44, bf16[256,8,88]{0,2,1:T(8,128)(2,1)S(1)} %bitcast.50, f32[256,8]{0,1:T(8,128)S(1)} %add_rsqrt_fusion), kind=kOutput, calls=%fused_computation.2 | convolution fusion | flops 3003660288 | bytes 81117184 | tf_op jit(solution)/shard_map/qhd,khd->hqk/dot_general | solution.py:57
  167.4 28.2 %fusion.30 = bf16[256,8,88]{0,2,1:T(8,128)(2,1)} fusion(bf16[8192,8,88]{0,2,1:T(8,128)(2,1)} %bitcast.43, f32[8,256,8192]{2,1,0:T(8,128)} %get-tuple-element.10, pred[256,8192]{1,0:T(8,128)(4,1)} %broadcast_compare_fusion, f32[256,8]{0,1:T(8,128)S(1)} %bitcast.56), kind=kOutput, calls=%fused_computation.48 | convolution fusion | flops 3003482112 | bytes 81108992 | tf_op jit(solution)/shard_map/hqk,khd->qhd/dot_general | solution.py:63
  195.6 2.1 fusion.82
  198.0 1.1 multiply_convert_fusion.1
  199.5 37.7 %all-gather.7.cloned.1.call-done = bf16[1024,1408]{1,0:T(8,128)(2,1)} async-done(((bf16[256,1408]{1,0:T(8,128)(2,1)}), bf16[1024,1408]{1,0:T(8,128)(2,1)}) %all-gather.7.cloned.1.call-update) | async-done | bytes 2883600 | tf_op jit(solution)/shard_map/all_gather | solution.py:81
  237.2 25.3 %convolution_convert_fusion.1 = bf16[1024,1408]{1,0:T(8,128)(2,1)} fusion(bf16[1536,1408]{1,0:T(8,128)(2,1)} %param.21, bf16[1024,1408]{1,0:T(8,128)(2,1)} %all-gather.7.cloned.1.call-done, bf16[1536,1408]{1,0:T(8,128)(2,1)} %param.19, f32[1536]{0:T(1024)S(1)} %convert_element_type.76), kind=kOutput, calls=%fused_computation.29 | convolution fusion | flops 8963620864 | bytes 14424064 | tf_op jit(solution)/shard_map/dot_general | solution.py:90
  262.6 0.3 all-gather.9.cloned.1.call-start
  263.5 35.6 %reduce-scatter.2.cloned.1.call-done = bf16[256,1408]{1,0:T(8,128)(2,1)} async-done(((bf16[1024,1408]{1,0:T(8,128)(2,1)}), bf16[256,1408]{1,0:T(8,128)(2,1)}) %reduce-scatter.2.cloned.1.call-update) | async-done | bytes 720912 | tf_op jit(solution)/shard_map/reduce_scatter | solution.py:89
  299.1 1.4 fusion.40
  300.5 1.5 multiply_reduce_fusion
  302.0 1.5 multiply_convert_fusion
  303.5 1.3 gather_fusion
  304.8 0.5 gather.7
  305.3 1.0 broadcast_select_fusion
  306.2 0.6 dynamic-slice
  307.8 5.3 %all-reduce = s32[256]{0:T(256)S(1)} all-reduce(s32[256]{0:T(256)S(1)} %add_dynamic-update-slice_fusion), channel_id=1, replica_groups=mesh['grp'=4,'tok'=32] {'grp'}, use_global_device_ids=true, to_apply=%add | all-reduce | flops 256 | bytes 2048
  313.2 30.3 %all-gather.9.cloned.1.call-done = bf16[256,5632]{1,0:T(8,128)(2,1)} async-done(((bf16[64,5632]{1,0:T(8,128)(2,1)}), bf16[256,5632]{1,0:T(8,128)(2,1)}) %all-gather.9.cloned.1.call-update) | async-done | bytes 2883600 | tf_op jit(solution)/shard_map/all_gather | solution.py:109
  343.5 5.3 %fusion.33 = bf16[256,512]{1,0:T(8,128)(2,1)S(1)} fusion(bf16[256,5632]{1,0:T(8,128)(2,1)} %all-gather.9.cloned.1.call-done, bf16[5632,512]{1,0:T(8,128)(2,1)} %param.24, f32[512]{0:T(512)S(1)} %copy-done.9), kind=kOutput, calls=%fused_computation.50 | convolution fusion | flops 1476657152 | bytes 8914944 | tf_op jit(solution)/shard_map/dot_general | solution.py:113
  348.8 0.3 fusion.26
  349.2 0.4 copy.17
  349.6 18.9 %all_to_all.15 = bf16[32,4,4,512]{3,2,1,0:T(4,128)(2,1)S(1)} all-to-all(bf16[32,4,4,512]{3,2,1,0:T(4,128)(2,1)S(1)} %copy.17), channel_id=1, replica_groups=mesh['grp'=4,'tok'=32] {'tok'}, dimensions={0} | all-to-all | bytes 1048576 | tf_op jit(solution)/shard_map/all_to_all | solution.py:127
  368.7 0.9 reshape.131
  (54 shorter events, 2.1 us)
Async XLA Ops:
  6.5 189.1 %copy-start = (bf16[704,1408]{1,0:T(8,128)(2,1)S(1)}, bf16[704,1408]{1,0:T(8,128)(2,1)}, u32[]{:S(2)}) copy-start(bf16[704,1408]{1,0:T(8,128)(2,1)} %param.18) | copy-start | bytes 5947396
  6.5 112.2 %all-gather.5.cloned.1.call-start = ((), (), s32[]{:S(2)}) async-start(), calls=%async_computation.2 | async-start | bytes 23789568 | tf_op jit(solution)/shard_map/all_gather | solution.py:51
  9.4 8.1 %copy-start.5 = (s32[256]{0:T(256)S(1)}, s32[256]{0:T(256)}, u32[]{:S(2)}) copy-start(s32[256]{0:T(256)} %param.14) | copy-start | bytes 3076
  14.3 1.0 copy-start.2
  17.5 219.8 %all-gather.7.cloned.1.call-start = ((), (), s32[]{:S(2)}) async-start(), calls=%async_computation.3 | async-start | bytes 3604480 | tf_op jit(solution)/shard_map/all_gather | solution.py:81
  195.6 3.8 %copy-start.6 = (bf16[1536]{0:T(1024)(128)(2,1)S(1)}, bf16[1536]{0:T(1024)(128)(2,1)}, u32[]{:S(2)}) copy-start(bf16[1536]{0:T(1024)(128)(2,1)} %param.20) | copy-start | bytes 9220
  199.2 99.9 %reduce-scatter.2.cloned.1.call-start = ((), (), s32[]{:S(2)}) async-start(), calls=%async_computation.4 | async-start | bytes 3604480 | tf_op jit(solution)/shard_map/reduce_scatter | solution.py:89
  199.5 63.4 %copy-start.7 = (s32[256]{0:T(256)S(1)}, s32[256]{0:T(256)}, u32[]{:S(2)}) copy-start(s32[256]{0:T(256)} %param.15) | copy-start | bytes 3076
  199.5 99.6 %copy-start.3 = (f32[1408]{0:T(1024)S(1)}, f32[1408]{0:T(1024)}, u32[]{:S(2)}) copy-start(f32[1408]{0:T(1024)} %param.22) | copy-start | bytes 16900
  262.5 39.4 %copy-start.4 = (f32[1408]{0:T(1024)S(1)}, f32[1408]{0:T(1024)}, u32[]{:S(2)}) copy-start(f32[1408]{0:T(1024)} %param.23) | copy-start | bytes 16900
  262.6 81.0 %all-gather.9.cloned.1.call-start = ((), (), s32[]{:S(2)}) async-start(), calls=%async_computation.5 | async-start | bytes 3604480 | tf_op jit(solution)/shard_map/all_gather | solution.py:109
  302.0 4.3 %copy-start.10 = (u32[128]{0:T(128)S(1)}, u32[128]{0:T(128)}, u32[]{:S(2)}) copy-start(u32[128]{0:T(128)} %constant.101) | copy-start | bytes 1540
  302.0 5.5 %copy-start.8 = (s32[64,1]{0,1:T(1,128)S(1)}, s32[64,1]{0,1:T(1,128)}, u32[]{:S(2)}) copy-start(s32[64,1]{0,1:T(1,128)} %param.16) | copy-start | bytes 772
  302.0 41.5 %copy-start.9 = (f32[512]{0:T(512)S(1)}, f32[512]{0:T(512)}, u32[]{:S(2)}) copy-start(f32[512]{0:T(512)} %param.25) | copy-start | bytes 6148
  343.5 26.1 %copy-start.1 = (bf16[704,1408]{1,0:T(8,128)(2,1)S(1)}, bf16[704,1408]{1,0:T(8,128)(2,1)}, u32[]{:S(2)}) copy-start(bf16[704,1408]{1,0:T(8,128)(2,1)} %param.18) | copy-start | bytes 5947396
Sparse Core Ops, SparseCore 0:
  17.6 101.0 all-gather.4
  199.3 37.8 all-gather.6
  262.7 36.3 reduce-scatter.1
  306.3 37.1 all-gather.8
where the time goes:
time: 377 us; the launch traced here: 376 us
  waiting for transfers between devices  176 us (47%)
  matrix products  98.3 us (26%)
  blocking collectives  50.2 us (13%)
  local copies, waits for them, and re-layouts  22.1 us (6%)
  other arithmetic  14.6 us (4%)
  between operations  14.1 us (4%)
    all_gather x1, waiting for transfers between devices, local(): piece_kv = lax.all_gather(keys_values, 'tok', axis=0, tiled=True)  72.6 us
    all_gather x1, waiting for transfers between devices, local(): lax.all_gather(mlp_in, 'grp', axis=0, tiled=True)  37.7 us
    reduce_scatter x1, waiting for transfers between devices, local(): lax.psum_scatter(jnp.dot(hidden, w_out, preferred_element_type=jnp.float3...  35.6 us
    dot_general x1, matrix products, local(): jnp.einsum('qhd,khd->hqk', queries, piece_keys, preferred_element_type=jn...  32.1 us
    all_gather x1, waiting for transfers between devices, local(): lax.all_gather(merged, 'grp', axis=0, tiled=True)  30.3 us
    dot_general x1, matrix products, local(): jnp.einsum('hqk,khd->qhd', weights.astype(jnp.bfloat16), piece_values, pr...  28.2 us
    all_gather x1, blocking collectives, local(): piece_seg = lax.all_gather(seg_ids, 'tok', axis=0, tiled=True)  26 us
    dot_general x1, matrix products, local(): jnp.dot(hidden, w_out, preferred_element_type=jnp.float32)  25.3 us
  transfers between devices with their start and end apart: 4, of which 4 were waited for; matrix products, arithmetic and copies ran while one was open for 1% of the time, Pallas kernels for 0%

commit v1 on v0

--- a/solution.py
+++ b/solution.py
@@ -124,7 +124,10 @@
         embedded.reshape(grp_devices, merged_count, out_cols),
         preferred_element_type=jnp.float32,
     ).astype(jnp.bfloat16)
-    received = lax.all_to_all(outgoing, "tok", split_axis=0, concat_axis=2, tiled=True)
+    received = jnp.concatenate(
+        lax.all_to_all(jnp.stack(jnp.split(outgoing, lax.axis_size("tok"), axis=0)), "tok", 0, 0),
+        axis=2,
+    )
     return received.reshape(grp_devices * tok_devices * slot_cap, out_cols)
 
 

time: 377 us -> 378 us (level)
  no operation moved by 1% of the time
where the time goes in v1:
time: 378 us; the launch traced here: 377 us
  waiting for transfers between devices  176 us (47%)
  matrix products  98.3 us (26%)
  blocking collectives  50.2 us (13%)
  local copies, waits for them, and re-layouts  23.3 us (6%)
  other arithmetic  14.6 us (4%)
  between operations  14.2 us (4%)
    all_gather x1, waiting for transfers between devices, local(): piece_kv = lax.all_gather(keys_values, 'tok', axis=0, tiled=True)  72.6 us
    all_gather x1, waiting for transfers between devices, local(): lax.all_gather(mlp_in, 'grp', axis=0, tiled=True)  37.7 us
    reduce_scatter x1, waiting for transfers between devices, local(): lax.psum_scatter(jnp.dot(hidden, w_out, preferred_element_type=jnp.float3...  35.6 us
    dot_general x1, matrix products, local(): jnp.einsum('qhd,khd->hqk', queries, piece_keys, preferred_element_type=jn...  32.1 us
    all_gather x1, waiting for transfers between devices, local(): lax.all_gather(merged, 'grp', axis=0, tiled=True)  30.3 us
    dot_general x1, matrix products, local(): jnp.einsum('hqk,khd->qhd', weights.astype(jnp.bfloat16), piece_values, pr...  28.2 us
    all_gather x1, blocking collectives, local(): piece_seg = lax.all_gather(seg_ids, 'tok', axis=0, tiled=True)  26 us
    dot_general x1, matrix products, local(): jnp.dot(hidden, w_out, preferred_element_type=jnp.float32)  25.3 us
  transfers between devices with their start and end apart: 4, of which 4 were waited for; matrix products, arithmetic and copies ran while one was open for 1% of the time, Pallas kernels for 0%

profile of v1, /device:TPU:1, one launch (start us, length us, event | category | flops | bytes accessed | tf_op | source)
XLA Modules:
  0.0 377.5 jit_solution(7121965196488820097)
XLA Ops:
  6.5 1.4 convert_reduce_fusion
  8.0 1.4 fusion.21
  9.4 4.9 %convolution_convert_fusion = bf16[256,2112]{0,1:T(8,128)(2,1)S(1)} fusion(bf16[1408,2112]{0,1:T(8,128)(2,1)} %param.17, bf16[256,1408]{1,0:T(8,128)(2,1)} %param.13, f32[256]{0:T(256)S(1)} %add_rsqrt_fusion.4, f32[256]{0:T(256)S(1)} %broadcast_multiply_fusion.2), kind=kOutput, calls=%fused_computation.28 | convolution fusion | flops 1524514816 | bytes 7751680 | tf_op jit(solution)/shard_map/dot_general | solution.py:40
  14.4 0.9 copy-done.2
  15.5 1.1 fusion.34
  16.5 0.9 pad_maximum_fusion
  17.5 26.0 %all-gather = s32[32,1,256]{2,1,0:T(1,128)S(1)} all-gather(s32[1,1,256]{2,1,0:T(1,128)S(1)} %bitcast.116), channel_id=1, replica_groups=mesh['grp'=4,'tok'=32] {'tok'}, dimensions={0}, use_global_device_ids=true | all-gather | bytes 33792 | tf_op jit(solution)/shard_map/all_gather | solution.py:52
  43.6 2.5 broadcast_compare_fusion
  46.1 72.6 %all-gather.5.cloned.1.call-done = bf16[8192,1408]{0,1:T(8,128)(2,1)} async-done(((bf16[256,1408]{0,1:T(8,128)(2,1)}), bf16[8192,1408]{0,1:T(8,128)(2,1)}) %all-gather.5.cloned.1.call-update) | async-done | bytes 23068688 | tf_op jit(solution)/shard_map/all_gather | solution.py:51
  118.7 16.6 %fusion.80 = (bf16[8192,704]{0,1:T(8,128)(2,1)}, bf16[8192,704]{0,1:T(8,128)(2,1)}) fusion(bf16[8192,1408]{0,1:T(8,128)(2,1)} %all-gather.5.cloned.1.call-done), kind=kLoop, calls=%fused_computation.148 | loop fusion | bytes 46137344 | tf_op jit(solution)/shard_map/slice | solution.py:54
  135.3 32.1 %fusion = (f32[8,256]{1,0:T(8,128)S(1)}, f32[8,256,8192]{2,1,0:T(8,128)}) fusion(pred[256,8192]{1,0:T(8,128)(4,1)} %broadcast_compare_fusion, bf16[8192,8,88]{0,2,1:T(8,128)(2,1)} %bitcast.106, bf16[256,8,88]{0,2,1:T(8,128)(2,1)S(1)} %bitcast.112, f32[256,8]{0,1:T(8,128)S(1)} %add_rsqrt_fusion), kind=kOutput, calls=%fused_computation.2 | convolution fusion | flops 3003660288 | bytes 81117184 | tf_op jit(solution)/shard_map/qhd,khd->hqk/dot_general | solution.py:57
  167.4 28.2 %fusion.30 = bf16[256,8,88]{0,2,1:T(8,128)(2,1)} fusion(bf16[8192,8,88]{0,2,1:T(8,128)(2,1)} %bitcast.105, f32[8,256,8192]{2,1,0:T(8,128)} %get-tuple-element.42, pred[256,8192]{1,0:T(8,128)(4,1)} %broadcast_compare_fusion, f32[256,8]{0,1:T(8,128)S(1)} %bitcast.118), kind=kOutput, calls=%fused_computation.48 | convolution fusion | flops 3003482112 | bytes 81108992 | tf_op jit(solution)/shard_map/hqk,khd->qhd/dot_general | solution.py:63
  195.6 2.1 fusion.84
  198.0 1.1 multiply_convert_fusion.1
  199.5 37.7 %all-gather.7.cloned.1.call-done = bf16[1024,1408]{1,0:T(8,128)(2,1)} async-done(((bf16[256,1408]{1,0:T(8,128)(2,1)}), bf16[1024,1408]{1,0:T(8,128)(2,1)}) %all-gather.7.cloned.1.call-update) | async-done | bytes 2883600 | tf_op jit(solution)/shard_map/all_gather | solution.py:81
  237.2 25.3 %convolution_convert_fusion.1 = bf16[1024,1408]{1,0:T(8,128)(2,1)} fusion(bf16[1536,1408]{1,0:T(8,128)(2,1)} %param.21, bf16[1024,1408]{1,0:T(8,128)(2,1)} %all-gather.7.cloned.1.call-done, bf16[1536,1408]{1,0:T(8,128)(2,1)} %param.19, f32[1536]{0:T(1024)S(1)} %convert_element_type.76), kind=kOutput, calls=%fused_computation.29 | convolution fusion | flops 8963620864 | bytes 14424064 | tf_op jit(solution)/shard_map/dot_general | solution.py:90
  263.5 35.6 %reduce-scatter.2.cloned.1.call-done = bf16[256,1408]{1,0:T(8,128)(2,1)} async-done(((bf16[1024,1408]{1,0:T(8,128)(2,1)}), bf16[256,1408]{1,0:T(8,128)(2,1)}) %reduce-scatter.2.cloned.1.call-update) | async-done | bytes 720912 | tf_op jit(solution)/shard_map/reduce_scatter | solution.py:89
  299.1 1.4 fusion.40
  300.5 1.5 multiply_reduce_fusion
  302.0 1.5 multiply_convert_fusion
  303.5 1.3 gather_fusion
  304.8 0.5 gather.7
  305.3 1.0 broadcast_select_fusion
  306.2 0.6 dynamic-slice
  307.8 5.3 %all-reduce = s32[256]{0:T(256)S(1)} all-reduce(s32[256]{0:T(256)S(1)} %add_dynamic-update-slice_fusion), channel_id=1, replica_groups=mesh['grp'=4,'tok'=32] {'grp'}, use_global_device_ids=true, to_apply=%add | all-reduce | flops 256 | bytes 2048
  313.2 30.3 %all-gather.9.cloned.1.call-done = bf16[256,5632]{1,0:T(8,128)(2,1)} async-done(((bf16[64,5632]{1,0:T(8,128)(2,1)}), bf16[256,5632]{1,0:T(8,128)(2,1)}) %all-gather.9.cloned.1.call-update) | async-done | bytes 2883600 | tf_op jit(solution)/shard_map/all_gather | solution.py:109
  343.5 5.3 %fusion.33 = bf16[256,512]{1,0:T(8,128)(2,1)S(1)} fusion(bf16[256,5632]{1,0:T(8,128)(2,1)} %all-gather.9.cloned.1.call-done, bf16[5632,512]{1,0:T(8,128)(2,1)} %param.24, f32[512]{0:T(512)S(1)} %copy-done.9), kind=kOutput, calls=%fused_computation.50 | convolution fusion | flops 1476657152 | bytes 8914944 | tf_op jit(solution)/shard_map/dot_general | solution.py:113
  348.8 0.3 fusion.26
  349.2 0.4 fusion.83
  349.6 0.7 fusion.82
  351.0 18.9 %all_to_all.5 = bf16[32,1,4,4,512]{4,3,2,1,0:T(4,128)(2,1)S(1)} all-to-all(bf16[32,1,4,4,512]{4,3,2,1,0:T(4,128)(2,1)S(1)} %constant_dynamic-update-slice_fusion), channel_id=1, replica_groups=mesh['grp'=4,'tok'=32] {'tok'}, dimensions={0} | all-to-all | bytes 1048576 | tf_op jit(solution)/shard_map/all_to_all | solution.py:128
  370.0 0.9 reshape_reshape.3
  (87 shorter events, 3.0 us)
Async XLA Ops:
  6.5 189.1 %copy-start = (bf16[704,1408]{1,0:T(8,128)(2,1)S(1)}, bf16[704,1408]{1,0:T(8,128)(2,1)}, u32[]{:S(2)}) copy-start(bf16[704,1408]{1,0:T(8,128)(2,1)} %param.18) | copy-start | bytes 5947396
  6.5 112.2 %all-gather.5.cloned.1.call-start = ((), (), s32[]{:S(2)}) async-start(), calls=%async_computation.2 | async-start | bytes 23789568 | tf_op jit(solution)/shard_map/all_gather | solution.py:51
  9.4 8.1 %copy-start.5 = (s32[256]{0:T(256)S(1)}, s32[256]{0:T(256)}, u32[]{:S(2)}) copy-start(s32[256]{0:T(256)} %param.14) | copy-start | bytes 3076
  14.3 1.0 copy-start.2
  17.5 219.8 %all-gather.7.cloned.1.call-start = ((), (), s32[]{:S(2)}) async-start(), calls=%async_computation.3 | async-start | bytes 3604480 | tf_op jit(solution)/shard_map/all_gather | solution.py:81
  195.6 3.8 %copy-start.6 = (bf16[1536]{0:T(1024)(128)(2,1)S(1)}, bf16[1536]{0:T(1024)(128)(2,1)}, u32[]{:S(2)}) copy-start(bf16[1536]{0:T(1024)(128)(2,1)} %param.20) | copy-start | bytes 9220
  199.2 99.9 %reduce-scatter.2.cloned.1.call-start = ((), (), s32[]{:S(2)}) async-start(), calls=%async_computation.4 | async-start | bytes 3604480 | tf_op jit(solution)/shard_map/reduce_scatter | solution.py:89
  199.5 63.4 %copy-start.7 = (s32[256]{0:T(256)S(1)}, s32[256]{0:T(256)}, u32[]{:S(2)}) copy-start(s32[256]{0:T(256)} %param.15) | copy-start | bytes 3076
  199.5 99.6 %copy-start.3 = (f32[1408]{0:T(1024)S(1)}, f32[1408]{0:T(1024)}, u32[]{:S(2)}) copy-start(f32[1408]{0:T(1024)} %param.22) | copy-start | bytes 16900
  262.5 39.4 %copy-start.4 = (f32[1408]{0:T(1024)S(1)}, f32[1408]{0:T(1024)}, u32[]{:S(2)}) copy-start(f32[1408]{0:T(1024)} %param.23) | copy-start | bytes 16900
  262.6 81.0 %all-gather.9.cloned.1.call-start = ((), (), s32[]{:S(2)}) async-start(), calls=%async_computation.5 | async-start | bytes 3604480 | tf_op jit(solution)/shard_map/all_gather | solution.py:109
  302.0 4.3 %copy-start.10 = (u32[128]{0:T(128)S(1)}, u32[128]{0:T(128)}, u32[]{:S(2)}) copy-start(u32[128]{0:T(128)} %constant.101) | copy-start | bytes 1540
  302.0 5.5 %copy-start.8 = (s32[64,1]{0,1:T(1,128)S(1)}, s32[64,1]{0,1:T(1,128)}, u32[]{:S(2)}) copy-start(s32[64,1]{0,1:T(1,128)} %param.16) | copy-start | bytes 772
  302.0 41.5 %copy-start.9 = (f32[512]{0:T(512)S(1)}, f32[512]{0:T(512)}, u32[]{:S(2)}) copy-start(f32[512]{0:T(512)} %param.25) | copy-start | bytes 6148
  343.5 27.4 %copy-start.1 = (bf16[704,1408]{1,0:T(8,128)(2,1)S(1)}, bf16[704,1408]{1,0:T(8,128)(2,1)}, u32[]{:S(2)}) copy-start(bf16[704,1408]{1,0:T(8,128)(2,1)} %param.18) | copy-start | bytes 5947396
Sparse Core Ops, SparseCore 0:
  17.6 101.0 all-gather.4
  199.3 37.8 all-gather.6
  262.7 36.3 reduce-scatter.1
  306.3 37.1 all-gather.8
